TPU v7x, 32 devices: a whole 2x2x4 slice. The times are simulated.
32 devices in a mesh: blk: 16 (over z, y, x), col: 2 (over core).
Axes of the slice: x: 2, y: 2, z: 4, core: 2. Of those that a mesh axis runs over, the one named last changes fastest.
Arguments:
- queries: bfloat16 [128, 16384], P('blk', 'col'), may hold values from -6 to 6
- factor: bfloat16 [16384, 1024], P('col', 'blk'), may hold values from -0.046875 to 0.046875
- eigenvalues: float32 [1024], replicated, may hold values from 0.05 to 20
- damping: float32 [1], replicated, may hold values from 0.5 to 2
- train_rows: bfloat16 [16384, 16384], P('blk', 'col'), may hold values from -0.046875 to 0.046875
Outputs:
- scores: bfloat16 [128, 16384], P('col', 'blk')
All inputs are finite; a program needn't handle non-finite values.
Results may differ from a plain program's by a relative error of at most 0.0049.
Values may be sent and summed in bfloat16 or wider, within the bound.
A program may use at most 64 MiB of HBM per device.

v0:
```python
import jax
import jax.numpy as jnp
from jax import lax
from jax.sharding import PartitionSpec as P


def per_device(queries, factor, eigenvalues, damping, train_rows):
    damp_value = damping[0]
    weights = eigenvalues / (eigenvalues + damp_value)
    query_part = lax.all_to_all(queries, "blk", split_axis=1, concat_axis=0, tiled=True)
    factor_part = lax.all_to_all(factor, "blk", split_axis=0, concat_axis=1, tiled=True)
    partial_value = jnp.dot(query_part, factor_part, preferred_element_type=jnp.float32)
    coefficient = lax.psum(partial_value, ("blk", "col"))
    scaled = coefficient * weights[None, :]
    correction = jnp.dot(scaled, factor_part.astype(jnp.float32).T, precision=lax.Precision.HIGHEST)
    pre_part = ((query_part.astype(jnp.float32) - correction) / damp_value).astype(jnp.bfloat16)
    pre_all = lax.all_gather(pre_part, "blk", axis=1, tiled=True)
    partial_scores = jnp.einsum(
        "qk,nk->qn", pre_all, train_rows, preferred_element_type=jnp.float32
    )
    scores = lax.psum_scatter(partial_scores, "col", scatter_dimension=0, tiled=True)
    return scores.astype(jnp.bfloat16)


def solution(mesh):
    in_specs = (P("blk", "col"), P("col", "blk"), P(), P(), P("blk", "col"))
    out_specs = P("col", "blk")
    return jax.shard_map(
        per_device, mesh=mesh, in_specs=in_specs, out_specs=out_specs, check_vma=False
    )
```

profile of v0, /device:TPU:0, one launch (start us, length us, event | category | flops | bytes accessed | tf_op | source)
XLA Modules:
  0.0 269.8 jit_solution(12998497539709083565)
XLA Ops:
  6.5 8.3 %all-to-all-start = ((bf16[8,16,512]{2,0,1:T(8,128)(2,1)}), bf16[8,16,512]{2,0,1:T(8,128)(2,1)S(1)}, u32[]{:S(2)}, u32[]{:S(2)}) async-start(bf16[8,16,512]{2,0,1:T(8,128)(2,1)} %bitcast.25), calls=%async_computation | async-start | bytes 262144 | tf_op jit(solution)/shard_map/all_to_all | solution.py:10
  14.9 0.0 all-reduce.2.cloned.1.call-start
  14.9 1.3 copy.10
  16.3 6.4 %all-to-all-done = bf16[8,16,512]{2,0,1:T(8,128)(2,1)S(1)} async-done(((bf16[8,16,512]{2,0,1:T(8,128)(2,1)}), bf16[8,16,512]{2,0,1:T(8,128)(2,1)S(1)}, u32[]{:S(2)}, u32[]{:S(2)}) %all-to-all-start) | async-done | bytes 131104 | tf_op jit(solution)/shard_map/all_to_all | solution.py:10
  22.7 28.3 %all_to_all.38 = bf16[16,512,64]{1,2,0:T(8,128)(2,1)S(1)} all-to-all(bf16[16,512,64]{1,2,0:T(8,128)(2,1)S(1)} %bitcast.21), channel_id=1, replica_groups=mesh['blk'=16,'col'=2] {'blk'}, dimensions={0} | all-to-all | bytes 2097152 | tf_op jit(solution)/shard_map/all_to_all | solution.py:11
  51.0 1.3 fusion.4
  52.3 0.0 all-reduce.2.cloned.1.call-update
  52.3 0.0 all-gather.2.cloned.1.call-start
  53.0 0.7 add_divide_fusion
  53.7 126.2 %all-reduce.2.cloned.1.call-done = f32[128,1024]{1,0:T(8,128)} async-done(((f32[128,1024]{1,0:T(8,128)}), f32[128,1024]{1,0:T(8,128)}) %all-reduce.2.cloned.1.call-update) | async-done | bytes 524304 | tf_op jit(solution)/shard_map/psum | solution.py:13
  179.9 2.3 fusion.1
  182.2 0.0 all-gather.2.cloned.1.call-update
  182.2 0.0 reduce-scatter.2.cloned.1.call-start
  182.2 60.3 %all-gather.2.cloned.1.call-done = bf16[128,8192]{1,0:T(8,128)(2,1)} async-done(((bf16[128,512]{1,0:T(8,128)(2,1)}), bf16[128,8192]{1,0:T(8,128)(2,1)}) %all-gather.2.cloned.1.call-update) | async-done | bytes 2097168 | tf_op jit(solution)/shard_map/all_gather | solution.py:17
  242.5 12.9 %fusion.6 = f32[128,1024]{1,0:T(8,128)} fusion(bf16[128,8192]{1,0:T(8,128)(2,1)} %all-gather.2.cloned.1.call-done, bf16[1024,8192]{1,0:T(8,128)(2,1)} %param.9), kind=kOutput, calls=%fused_computation.9 | convolution fusion | flops 2147483648 | bytes 19398656 | tf_op jit(solution)/shard_map/qk,nk->qn/dot_general | solution.py:18
  255.4 0.0 reduce-scatter.2.cloned.1.call-update
  255.4 6.3 %reduce-scatter.2.cloned.1.call-done = f32[64,1024]{1,0:T(8,128)} async-done(((f32[128,1024]{1,0:T(8,128)}), f32[64,1024]{1,0:T(8,128)}) %reduce-scatter.2.cloned.1.call-update) | async-done | bytes 262160 | tf_op jit(solution)/shard_map/reduce_scatter | solution.py:21
  261.7 1.6 convert_element_type.12
Async XLA Ops:
  6.5 16.1 %all-to-all-start = ((bf16[8,16,512]{2,0,1:T(8,128)(2,1)}), bf16[8,16,512]{2,0,1:T(8,128)(2,1)S(1)}, u32[]{:S(2)}, u32[]{:S(2)}) async-start(bf16[8,16,512]{2,0,1:T(8,128)(2,1)} %bitcast.25), calls=%async_computation | async-start | bytes 262144 | tf_op jit(solution)/shard_map/all_to_all | solution.py:10
  14.9 165.0 %all-reduce.2.cloned.1.call-start = ((), (), s32[]{:S(2)}) async-start(), calls=%async_computation.3 | async-start | bytes 1048576 | tf_op jit(solution)/shard_map/psum | solution.py:13
  52.3 190.2 %all-gather.2.cloned.1.call-start = ((), (), s32[]{:S(2)}) async-start(), calls=%async_computation.4 | async-start | bytes 2228224 | tf_op jit(solution)/shard_map/all_gather | solution.py:17
  182.2 79.5 %reduce-scatter.2.cloned.1.call-start = ((), (), s32[]{:S(2)}) async-start(), calls=%async_computation.5 | async-start | bytes 786432 | tf_op jit(solution)/shard_map/reduce_scatter | solution.py:21
Sparse Core Ops, SparseCore 0:
  52.4 127.3 all-reduce.1
  182.6 59.8 all-gather.1
  255.6 6.0 reduce-scatter.1
where the time goes:
time: 270 us
  waiting for transfers between devices  199 us (74%)
  blocking collectives  28.3 us (10%)
  matrix products  16.4 us (6%)
  between operations  13.8 us (5%)
  starting transfers between devices  8.47 us (3%)
    psum x1, waiting for transfers between devices, per_device(): coefficient = lax.psum(partial_value, ('blk', 'col'))  126 us
    all_gather x1, waiting for transfers between devices, per_device(): pre_all = lax.all_gather(pre_part, 'blk', axis=1, tiled=True)  60.3 us
    all_to_all x1, blocking collectives, per_device(): lax.all_to_all(factor, 'blk', split_axis=0, concat_axis=1, tiled=True)  28.3 us
    dot_general x1, matrix products, per_device(): jnp.einsum('qk,nk->qn', pre_all, train_rows, preferred_element_type=jnp.f...  12.9 us
    all_to_all x1, starting transfers between devices, per_device(): lax.all_to_all(queries, 'blk', split_axis=1, concat_axis=0, tiled=True)  8.34 us
    all_to_all x1, waiting for transfers between devices, per_device(): lax.all_to_all(queries, 'blk', split_axis=1, concat_axis=0, tiled=True)  6.41 us
    reduce_scatter x1, waiting for transfers between devices, per_device(): lax.psum_scatter(partial_scores, 'col', scatter_dimension=0, tiled=True)  6.26 us
  transfers between devices with their start and end apart: 4, of which 4 were waited for; matrix products, arithmetic and copies ran while one was open for 1% of the time, Pallas kernels for 0%

commit v1 on v0

--- a/solution.py
+++ b/solution.py
@@ -10,7 +10,7 @@
     query_part = lax.all_to_all(queries, "blk", split_axis=1, concat_axis=0, tiled=True)
     factor_part = lax.all_to_all(factor, "blk", split_axis=0, concat_axis=1, tiled=True)
     partial_value = jnp.dot(query_part, factor_part, preferred_element_type=jnp.float32)
-    coefficient = lax.psum(partial_value, ("blk", "col"))
+    coefficient = lax.psum(lax.psum(partial_value, "col"), "blk")
     scaled = coefficient * weights[None, :]
     correction = jnp.dot(scaled, factor_part.astype(jnp.float32).T, precision=lax.Precision.HIGHEST)
     pre_part = ((query_part.astype(jnp.float32) - correction) / damp_value).astype(jnp.bfloat16)

time: 270 us -> 275 us (1.019)
  waiting for transfers between devices: 199 us -> 204 us
    psum x1 -> x2, waiting for transfers between devices: 126 us -> 131 us  [per_device(): coefficient = lax.psum(lax.psum(partial_value, 'col'), 'blk')]
  transfers between devices with their start and end apart: 4 -> 5, of which waited for: 4 -> 5; matrix products, arithmetic and copies ran while one was open for 1% -> 1% of each run, Pallas kernels for 0% -> 0%
where the time goes in v1:
time: 275 us
  waiting for transfers between devices  204 us (74%)
  blocking collectives  28.3 us (10%)
  matrix products  16.4 us (6%)
  between operations  13.8 us (5%)
  starting transfers between devices  8.5 us (3%)
    psum x2, waiting for transfers between devices, per_device(): coefficient = lax.psum(lax.psum(partial_value, 'col'), 'blk')  131 us
    all_gather x1, waiting for transfers between devices, per_device(): pre_all = lax.all_gather(pre_part, 'blk', axis=1, tiled=True)  60.3 us
    all_to_all x1, blocking collectives, per_device(): lax.all_to_all(factor, 'blk', split_axis=0, concat_axis=1, tiled=True)  28.3 us
    dot_general x1, matrix products, per_device(): jnp.einsum('qk,nk->qn', pre_all, train_rows, preferred_element_type=jnp.f...  12.9 us
    all_to_all x1, starting transfers between devices, per_device(): lax.all_to_all(queries, 'blk', split_axis=1, concat_axis=0, tiled=True)  8.34 us
    all_to_all x1, waiting for transfers between devices, per_device(): lax.all_to_all(queries, 'blk', split_axis=1, concat_axis=0, tiled=True)  6.41 us
    reduce_scatter x1, waiting for transfers between devices, per_device(): lax.psum_scatter(partial_scores, 'col', scatter_dimension=0, tiled=True)  6.26 us
  transfers between devices with their start and end apart: 5, of which 5 were waited for; matrix products, arithmetic and copies ran while one was open for 1% of the time, Pallas kernels for 0%

profile of v1, /device:TPU:0, one launch (start us, length us, event | category | flops | bytes accessed | tf_op | source)
XLA Modules:
  0.0 274.9 jit_solution(5992573453162692020)
XLA Ops:
  6.5 8.3 %all-to-all-start = ((bf16[8,16,512]{2,0,1:T(8,128)(2,1)}), bf16[8,16,512]{2,0,1:T(8,128)(2,1)S(1)}, u32[]{:S(2)}, u32[]{:S(2)}) async-start(bf16[8,16,512]{2,0,1:T(8,128)(2,1)} %bitcast.25), calls=%async_computation | async-start | bytes 262144 | tf_op jit(solution)/shard_map/all_to_all | solution.py:10
  14.9 0.0 all-reduce.3.cloned.1.call-start
  14.9 1.3 copy.10
  16.3 6.4 %all-to-all-done = bf16[8,16,512]{2,0,1:T(8,128)(2,1)S(1)} async-done(((bf16[8,16,512]{2,0,1:T(8,128)(2,1)}), bf16[8,16,512]{2,0,1:T(8,128)(2,1)S(1)}, u32[]{:S(2)}, u32[]{:S(2)}) %all-to-all-start) | async-done | bytes 131104 | tf_op jit(solution)/shard_map/all_to_all | solution.py:10
  22.7 28.3 %all_to_all.38 = bf16[16,512,64]{1,2,0:T(8,128)(2,1)S(1)} all-to-all(bf16[16,512,64]{1,2,0:T(8,128)(2,1)S(1)} %bitcast.21), channel_id=1, replica_groups=mesh['blk'=16,'col'=2] {'blk'}, dimensions={0} | all-to-all | bytes 2097152 | tf_op jit(solution)/shard_map/all_to_all | solution.py:11
  51.0 1.3 fusion.4
  52.3 0.0 all-reduce.3.cloned.1.call-update
  52.3 0.0 all-reduce.5.cloned.1.call-start
  52.4 17.1 %all-reduce.3.cloned.1.call-done = f32[128,1024]{1,0:T(8,128)} async-done(((f32[128,1024]{1,0:T(8,128)}), f32[128,1024]{1,0:T(8,128)}) %all-reduce.3.cloned.1.call-update) | async-done | bytes 524304 | tf_op jit(solution)/shard_map/psum | solution.py:13
  69.4 0.0 all-reduce.5.cloned.1.call-update
  69.5 0.0 all-gather.2.cloned.1.call-start
  70.2 0.7 add_divide_fusion
  70.9 114.1 %all-reduce.5.cloned.1.call-done = f32[128,1024]{1,0:T(8,128)} async-done(((f32[128,1024]{1,0:T(8,128)}), f32[128,1024]{1,0:T(8,128)}) %all-reduce.5.cloned.1.call-update) | async-done | bytes 524304 | tf_op jit(solution)/shard_map/psum | solution.py:13
  184.9 2.3 fusion.1
  187.2 0.0 all-gather.2.cloned.1.call-update
  187.3 0.0 reduce-scatter.2.cloned.1.call-start
  187.3 60.3 %all-gather.2.cloned.1.call-done = bf16[128,8192]{1,0:T(8,128)(2,1)} async-done(((bf16[128,512]{1,0:T(8,128)(2,1)}), bf16[128,8192]{1,0:T(8,128)(2,1)}) %all-gather.2.cloned.1.call-update) | async-done | bytes 2097168 | tf_op jit(solution)/shard_map/all_gather | solution.py:17
  247.6 12.9 %fusion.6 = f32[128,1024]{1,0:T(8,128)} fusion(bf16[128,8192]{1,0:T(8,128)(2,1)} %all-gather.2.cloned.1.call-done, bf16[1024,8192]{1,0:T(8,128)(2,1)} %param.9), kind=kOutput, calls=%fused_computation.9 | convolution fusion | flops 2147483648 | bytes 19398656 | tf_op jit(solution)/shard_map/qk,nk->qn/dot_general | solution.py:18
  260.5 0.0 reduce-scatter.2.cloned.1.call-update
  260.5 6.3 %reduce-scatter.2.cloned.1.call-done = f32[64,1024]{1,0:T(8,128)} async-done(((f32[128,1024]{1,0:T(8,128)}), f32[64,1024]{1,0:T(8,128)}) %reduce-scatter.2.cloned.1.call-update) | async-done | bytes 262160 | tf_op jit(solution)/shard_map/reduce_scatter | solution.py:21
  266.7 1.6 convert_element_type.12
Async XLA Ops:
  6.5 16.1 %all-to-all-start = ((bf16[8,16,512]{2,0,1:T(8,128)(2,1)}), bf16[8,16,512]{2,0,1:T(8,128)(2,1)S(1)}, u32[]{:S(2)}, u32[]{:S(2)}) async-start(bf16[8,16,512]{2,0,1:T(8,128)(2,1)} %bitcast.25), calls=%async_computation | async-start | bytes 262144 | tf_op jit(solution)/shard_map/all_to_all | solution.py:10
  14.9 54.6 %all-reduce.3.cloned.1.call-start = ((), (), s32[]{:S(2)}) async-start(), calls=%async_computation.3 | async-start | bytes 1048576 | tf_op jit(solution)/shard_map/psum | solution.py:13
  52.3 132.6 %all-reduce.5.cloned.1.call-start = ((), (), s32[]{:S(2)}) async-start(), calls=%async_computation.4 | async-start | bytes 1048576 | tf_op jit(solution)/shard_map/psum | solution.py:13
  69.5 178.1 %all-gather.2.cloned.1.call-start = ((), (), s32[]{:S(2)}) async-start(), calls=%async_computation.5 | async-start | bytes 2228224 | tf_op jit(solution)/shard_map/all_gather | solution.py:17
  187.3 79.5 %reduce-scatter.2.cloned.1.call-start = ((), (), s32[]{:S(2)}) async-start(), calls=%async_computation.6 | async-start | bytes 786432 | tf_op jit(solution)/shard_map/reduce_scatter | solution.py:21
Sparse Core Ops, SparseCore 0:
  52.4 16.9 all-reduce.2
  74.6 110.3 all-reduce.4
  187.7 59.8 all-gather.1
  260.6 6.0 reduce-scatter.1
